TPU v7x, 128 devices: a whole 4x4x4 slice. The times are simulated.
128 devices in a mesh: dp: 32 (over y, x, core), fsdp: 4 (over z).
Axes of the slice: x: 4, y: 4, z: 4, core: 2. Of those that a mesh axis runs over, the one named last changes fastest.
Arguments:
- memory: bfloat16 [16384, 4096], P('dp'), may hold values from -6 to 6
- key_weight: bfloat16 [4096, 2048], P('dp', 'fsdp'), may hold values from -0.09375 to 0.09375
- value_weight: bfloat16 [4096, 2048], P('dp', 'fsdp'), may hold values from -0.09375 to 0.09375
- query: bfloat16 [16384, 2048], P('dp', 'fsdp')
- grad_context: bfloat16 [16384, 2048], P('dp', 'fsdp')
- target_segment: int32 [32, 512], P('dp'), may hold values from 0 to 31, never falling along the last dimension, each value on 1 to 32 neighbouring positions
- memory_segment: int32 [32, 512], P('dp'), may hold values from 0 to 31, never falling along the last dimension, each value on 1 to 128 neighbouring positions
- example_pack: int32 [32, 32], replicated, may hold values from 0 to 31, as said below
- example_slot: int32 [32, 32], replicated, may hold values from 0 to 31, as said below
Outputs:
- context: bfloat16 [16384, 2048], P('dp', 'fsdp')
- grad_query: bfloat16 [16384, 2048], P('dp', 'fsdp')
- grad_key_weight: float32 [4096, 2048], P('dp', 'fsdp')
- grad_value_weight: float32 [4096, 2048], P('dp', 'fsdp')
- grad_memory: bfloat16 [16384, 4096], P(('dp', 'fsdp'))
Inputs may be any that keep to these rules, and one draw needn't show every extreme that they name: `target_segment`: rows of each target pack are ordered by example; every one of the 32 examples has 1 to 32 decoder rows, and some example has exactly 32. `memory_segment`: rows of each input pack are ordered by segment; every one of the 32 segments has 1 to 128 memory rows, and some segment has exactly 128. `example_pack`: the 32 examples of one target pack have their memory in 32 different input packs, and every input pack holds the memory of exactly 32 examples. `example_slot`: the examples whose memory lies in one input pack carry the segment numbers 0 to 31 of that pack, each once.
All inputs are finite; a program needn't handle non-finite values.
Results may differ from a plain program's by a relative error of at most 0.017.
Values may be sent and summed in bfloat16 or wider, within the bound.
No kernel may reach another device: no remote copies, remote signals or barrier semaphores. Data moves between devices by JAX's collectives and lax.ppermute only.
A program may use at most 128 MiB of HBM per device.

v0:
```python
import jax
import jax.numpy as jnp
from jax import lax
from jax.sharding import PartitionSpec as P

HD = 256
SCORE_SCALE = 0.0625
MASKED_SCORE = -1e30


def lookup(table, indices):
    positions = jnp.arange(table.shape[0], dtype=jnp.int32)
    return jnp.sum(jnp.where(indices[..., None] == positions, table, 0), axis=-1)


def slot_layout(segment, my_packs, peer_count, depth):
    example_ids = jnp.arange(my_packs.shape[0], dtype=jnp.int32)
    member = (segment[None, :] == example_ids[:, None]).astype(jnp.int32)
    counts = jnp.sum(member, axis=1)
    starts = jnp.cumsum(counts) - counts
    peer_ids = jnp.arange(peer_count, dtype=jnp.int32)
    matched = my_packs[None, :] == peer_ids[:, None]
    chosen = jnp.sum(jnp.where(matched, example_ids[None, :], 0), axis=1)
    present = jnp.any(matched, axis=1)
    offsets = jnp.arange(depth, dtype=jnp.int32)
    live = present[:, None] & (offsets[None, :] < lookup(counts, chosen)[:, None])
    source = jnp.where(live, lookup(starts, chosen)[:, None] + offsets[None, :], 0)
    positions = jnp.arange(segment.shape[0], dtype=jnp.int32)
    target_slot = lookup(my_packs, segment) * depth + positions - lookup(starts, segment)
    return (source, live, target_slot)


def to_slots(row_data, source, live):
    peer_count, depth = source.shape
    taken = jnp.take(row_data, source.reshape(-1), axis=0).reshape(
        peer_count, depth, row_data.shape[1]
    )
    return jnp.where(live[..., None], taken, jnp.zeros_like(taken))


def from_slots(slot_data, target_slot):
    flat_data = slot_data.reshape(-1, slot_data.shape[2])
    return jnp.take(flat_data, target_slot, axis=0)


def pair_scores(left, key_set):
    return jnp.einsum("trhd,khd->thrk", left, key_set, preferred_element_type=jnp.float32)


def apply_weights(weights, value_set):
    return jnp.einsum("thrk,khd->trhd", weights, value_set, preferred_element_type=jnp.float32)


def spread_back(weights, right):
    return jnp.einsum("thrk,trhd->khd", weights, right, preferred_element_type=jnp.float32)


def softmax_weights(query_set, key_set, valid):
    scores = pair_scores(query_set, key_set) * SCORE_SCALE
    scores = jnp.where(valid[:, None, None, :], scores, MASKED_SCORE)
    row_top = jnp.max(scores, axis=-1, keepdims=True)
    raised = jnp.exp(scores - row_top)
    return raised / jnp.sum(raised, axis=-1, keepdims=True)


def per_device(
    memory,
    key_weight,
    value_weight,
    query,
    grad_context,
    target_segment,
    memory_segment,
    example_pack,
    example_slot,
):
    peer_count = lax.axis_size("dp")
    my_index = lax.axis_index("dp")
    width = key_weight.shape[1]
    heads = width // HD
    row_count = memory.shape[0]
    depth = 2 * query.shape[0] // peer_count
    stacked = jnp.stack((key_weight, value_weight), axis=1)
    piece = lax.all_gather(stacked, "dp", axis=0, tiled=True)
    columns = memory
    projected = jnp.dot(
        columns, piece.reshape(piece.shape[0], 2 * width), preferred_element_type=jnp.float32
    )
    key_rows = projected[:, :width].astype(jnp.bfloat16).reshape(row_count, heads, HD)
    value_rows = projected[:, width:].astype(jnp.bfloat16).reshape(row_count, heads, HD)
    mem_segment = memory_segment[0]
    owned = example_pack == my_index
    wanted = jnp.where(
        jnp.any(owned, axis=1), jnp.sum(jnp.where(owned, example_slot, 0), axis=1), -1
    )
    valid = mem_segment[None, :] == wanted[:, None]
    my_packs = lax.dynamic_index_in_dim(example_pack, my_index, 0, keepdims=False)
    source, live, target_slot = slot_layout(target_segment[0], my_packs, peer_count, depth)
    outgoing = to_slots(query, source, live)
    piece = lax.all_to_all(outgoing, "dp", split_axis=0, concat_axis=0, tiled=True)
    query_set = piece.reshape(peer_count, piece.shape[1], heads, HD)
    weights = softmax_weights(query_set, key_rows, valid).astype(jnp.bfloat16)
    mixed = apply_weights(weights, value_rows)
    answers = mixed.astype(jnp.bfloat16).reshape(peer_count, piece.shape[1], width)
    arrived = piece
    returned = lax.all_to_all(answers, "dp", split_axis=0, concat_axis=0, tiled=True)
    context = from_slots(returned, target_slot)
    grad_outgoing = to_slots(grad_context, source, live)
    grad_arrived = lax.all_to_all(grad_outgoing, "dp", split_axis=0, concat_axis=0, tiled=True)
    query_set = arrived.reshape(peer_count, depth, heads, HD)
    grad_set = grad_arrived.reshape(peer_count, depth, heads, HD)
    probability = softmax_weights(query_set, key_rows, valid)
    rounded = probability.astype(jnp.bfloat16)
    grad_prob = pair_scores(grad_set, value_rows)
    row_delta = jnp.sum(probability * grad_prob, axis=-1, keepdims=True)
    grad_scores = (probability * (grad_prob - row_delta) * SCORE_SCALE).astype(jnp.bfloat16)
    slot_grad = (
        apply_weights(grad_scores, key_rows).astype(jnp.bfloat16).reshape(peer_count, depth, width)
    )
    grad_returned = lax.all_to_all(slot_grad, "dp", split_axis=0, concat_axis=0, tiled=True)
    grad_query = from_slots(grad_returned, target_slot)
    grad_keys = spread_back(grad_scores, query_set)
    grad_values = spread_back(rounded, grad_set)
    grad_kv = jnp.concatenate(
        [
            grad_keys.astype(jnp.bfloat16).reshape(row_count, width),
            grad_values.astype(jnp.bfloat16).reshape(row_count, width),
        ],
        axis=1,
    )
    columns = memory
    weight_grads = lax.psum_scatter(
        lax.dot_general(
            columns, grad_kv, (((0,), (0,)), ((), ())), preferred_element_type=jnp.float32
        ).astype(jnp.bfloat16),
        "dp",
        scatter_dimension=0,
        tiled=True,
    ).astype(jnp.float32)
    piece = lax.all_gather(stacked, "dp", axis=0, tiled=True)
    flat_piece = piece.reshape(piece.shape[0], 2 * width)
    partial_sums = lax.dot_general(
        grad_kv, flat_piece, (((1,), (1,)), ((), ())), preferred_element_type=jnp.float32
    )
    grad_memory = lax.psum_scatter(partial_sums, "fsdp", scatter_dimension=0, tiled=True)
    return (
        context,
        grad_query,
        weight_grads[:, :width],
        weight_grads[:, width:],
        grad_memory.astype(jnp.bfloat16),
    )


def solution(mesh):
    placed = (
        P("dp", None),
        P("dp", "fsdp"),
        P("dp", "fsdp"),
        P("dp", "fsdp"),
        P("dp", "fsdp"),
        P("dp", None),
        P("dp", None),
        P(),
        P(),
    )
    return jax.shard_map(
        per_device,
        mesh=mesh,
        in_specs=placed,
        out_specs=(
            P("dp", "fsdp"),
            P("dp", "fsdp"),
            P("dp", "fsdp"),
            P("dp", "fsdp"),
            P(("dp", "fsdp"), None),
        ),
        check_vma=False,
    )
```

profile of v0, /device:TPU:1, one launch (start us, length us, event | category | flops | bytes accessed | tf_op | source)
XLA Modules:
  0.0 347.4 jit_solution(4169301897632804495)
XLA Ops:
  12.5 4.0 %gather_fusion.2 = bf16[1024,512]{1,0:T(8,128)(2,1)S(1)} fusion(bf16[512,512]{1,0:T(8,128)(2,1)S(1)} %copy-done, s32[1024]{0:T(1024)S(1)} %fusion.35), kind=kCustom, calls=%fused_computation.2.clone | custom fusion | bytes 2101248 | tf_op jit(solution)/shard_map/jit(_take)/gather | solution.py:35
  16.5 4.0 %gather_fusion = bf16[1024,512]{1,0:T(8,128)(2,1)S(1)} fusion(bf16[512,512]{1,0:T(8,128)(2,1)S(1)} %copy-done.2, s32[1024]{0:T(1024)S(1)} %fusion.35), kind=kCustom, calls=%fused_computation.clone | custom fusion | bytes 2101248 | tf_op jit(solution)/shard_map/jit(_take)/gather | solution.py:35
  22.0 26.2 %all_to_all.20 = bf16[32,32,512]{2,1,0:T(8,128)(2,1)S(1)} all-to-all(bf16[32,32,512]{2,1,0:T(8,128)(2,1)S(1)} %get-tuple-element.40), channel_id=1, replica_groups=mesh['dp'=32,'fsdp'=4] {'dp'}, dimensions={0} | all-to-all | bytes 2097152 | tf_op jit(solution)/shard_map/all_to_all | solution.py:100
  48.3 4.4 %all-to-all-start.2 = ((bf16[32,32,512]{2,1,0:T(8,128)(2,1)}), bf16[32,32,512]{2,1,0:T(8,128)(2,1)S(1)}, u32[]{:S(2)}, u32[]{:S(2)}) async-start(bf16[32,32,512]{2,1,0:T(8,128)(2,1)} %get-tuple-element.39), calls=%async_computation.2 | async-start | bytes 2097152 | tf_op jit(solution)/shard_map/all_to_all | solution.py:109
  54.5 19.9 %all-to-all-done.2 = bf16[32,32,512]{2,1,0:T(8,128)(2,1)S(1)} async-done(((bf16[32,32,512]{2,1,0:T(8,128)(2,1)}), bf16[32,32,512]{2,1,0:T(8,128)(2,1)S(1)}, u32[]{:S(2)}, u32[]{:S(2)}) %all-to-all-start.2) | async-done | bytes 1048608 | tf_op jit(solution)/shard_map/all_to_all | solution.py:109
  75.5 17.4 %all-gather.2.cloned.1.call-done = bf16[4096,2,512]{0,2,1:T(8,128)(2,1)} async-done(((bf16[128,2,512]{0,2,1:T(8,128)(2,1)}), bf16[4096,2,512]{0,2,1:T(8,128)(2,1)}) %all-gather.2.cloned.1.call-update) | async-done | bytes 8388624 | tf_op jit(solution)/shard_map/all_gather | solution.py:84
  92.9 9.2 %fusion.19 = bf16[512,1024]{0,1:T(8,128)(2,1)S(1)} fusion(bf16[4096,1024]{0,1:T(8,128)(2,1)} %bitcast.94, bf16[512,4096]{1,0:T(8,128)(2,1)} %param.13), kind=kOutput, calls=%fused_computation.23 | convolution fusion | flops 4295491584 | bytes 13631488 | tf_op jit(solution)/shard_map/dot_general | solution.py:86
  102.2 2.7 fusion.48
  105.6 6.1 %fusion.46 = (f32[32,2,32]{2,0,1:T(8,128)S(1)}, f32[32,2,32,512]{3,2,0,1:T(8,128)S(1)}) fusion(f32[2,512,32,32]{1,3,2,0:T(8,128)S(1)} %bitcast.100, pred[32,512]{1,0:T(8,128)(4,1)S(1)} %broadcast_compare_fusion), kind=kOutput, calls=%fused_computation.77 | output fusion | flops 6291967 | bytes 8413184 | tf_op jit(solution)/shard_map/sub | solution.py:62
  111.6 2.2 fusion.26
  113.8 15.8 %fusion.27 = bf16[2,256,512]{2,1,0:T(8,128)(2,1)S(1)} fusion(f32[32,2,32,512]{3,2,0,1:T(8,128)} %bitcast.98, bf16[32,4,2,8,256]{4,3,2,1,0:T(8,128)(2,1)S(1)} %bitcast.102, f32[32,2,32,512]{3,2,0,1:T(8,128)} %copy-done.10, f32[32,2,32]{2,0,1:T(8,128)S(1)} %get-tuple-element.45), kind=kOutput, calls=%fused_computation.28 | convolution fusion | flops 544475648 | bytes 9969664 | tf_op jit(solution)/shard_map/thrk,trhd->khd/dot_general | solution.py:55
  129.7 9.6 %convert_bitcast_fusion = bf16[4096,1024]{0,1:T(8,128)(2,1)} fusion(bf16[512,4096]{1,0:T(8,128)(2,1)} %param.13, bf16[512,512]{0,1:T(8,128)(2,1)S(1)} %bitcast.112, bf16[512,512]{0,1:T(8,128)(2,1)S(1)} %bitcast.114), kind=kOutput, calls=%fused_computation.6 | convolution fusion | flops 4301258752 | bytes 13631488 | tf_op jit(solution)/shard_map/dot_general | solution.py:133
  139.3 11.9 %copy.82 = bf16[4096,1024]{1,0:T(8,128)(2,1)} copy(bf16[4096,1024]{0,1:T(8,128)(2,1)} %convert_bitcast_fusion) | data formatting | bytes 16777216
  151.5 10.2 %fusion.32 = f32[512,4096]{1,0:T(8,128)} fusion(bf16[4096,1024]{0,1:T(8,128)(2,1)} %bitcast.95, bf16[512,512]{0,1:T(8,128)(2,1)S(1)} %bitcast.113, bf16[512,512]{0,1:T(8,128)(2,1)S(1)} %bitcast.115), kind=kOutput, calls=%fused_computation.38 | convolution fusion | flops 4297064448 | bytes 17825792 | tf_op jit(solution)/shard_map/dot_general | solution.py:142
  161.7 17.8 %fusion.20 = bf16[2,32,4,8,256]{4,3,2,1,0:T(8,128)(2,1)S(1)} fusion(bf16[512,2,256,1]{0,2,3,1:T(8,128)(2,1)S(1)} %bitcast.111, f32[32,2,32,512]{3,2,0,1:T(8,128)} %bitcast.99, f32[32,2,32,512]{3,2,0,1:T(8,128)} %copy-done.10, f32[32,2,32]{2,0,1:T(8,128)S(1)} %get-tuple-element.45), kind=kOutput, calls=%fused_computation.24 | convolution fusion | flops 544737792 | bytes 9969664 | tf_op jit(solution)/shard_map/thrk,khd->trhd/dot_general | solution.py:51
  180.6 5.5 %all-to-all-start.3 = ((bf16[32,32,512]{2,1,0:T(8,128)(2,1)}), bf16[32,32,512]{2,1,0:T(8,128)(2,1)S(1)}, u32[]{:S(2)}, u32[]{:S(2)}) async-start(bf16[32,32,512]{2,1,0:T(8,128)(2,1)} %bitcast.54), calls=%async_computation.3 | async-start | bytes 2097152 | tf_op jit(solution)/shard_map/all_to_all | solution.py:120
  186.1 3.2 fusion.18
  190.3 12.9 %all-to-all-done.3 = bf16[32,32,512]{2,1,0:T(8,128)(2,1)S(1)} async-done(((bf16[32,32,512]{2,1,0:T(8,128)(2,1)}), bf16[32,32,512]{2,1,0:T(8,128)(2,1)S(1)}, u32[]{:S(2)}, u32[]{:S(2)}) %all-to-all-start.3) | async-done | bytes 1048608 | tf_op jit(solution)/shard_map/all_to_all | solution.py:120
  203.3 4.0 %all-to-all-start.1 = ((bf16[32,32,512]{2,1,0:T(8,128)(2,1)}), bf16[32,32,512]{2,1,0:T(8,128)(2,1)S(1)}, u32[]{:S(2)}, u32[]{:S(2)}) async-start(bf16[32,32,512]{2,1,0:T(8,128)(2,1)} %bitcast.105), calls=%async_computation.1 | async-start | bytes 2097152 | tf_op jit(solution)/shard_map/all_to_all | solution.py:106
  207.4 2.0 gather_fusion.3
  209.4 23.8 %all-to-all-done.1 = bf16[32,32,512]{2,1,0:T(8,128)(2,1)S(1)} async-done(((bf16[32,32,512]{2,1,0:T(8,128)(2,1)}), bf16[32,32,512]{2,1,0:T(8,128)(2,1)S(1)}, u32[]{:S(2)}, u32[]{:S(2)}) %all-to-all-start.1) | async-done | bytes 1048608 | tf_op jit(solution)/shard_map/all_to_all | solution.py:106
  236.2 17.4 %reduce-scatter.7.cloned.1.call-done = bf16[128,1024]{1,0:T(8,128)(2,1)} async-done(((bf16[4096,1024]{1,0:T(8,128)(2,1)}), bf16[128,1024]{1,0:T(8,128)(2,1)}) %reduce-scatter.7.cloned.1.call-update) | async-done | bytes 262160
  256.5 81.6 %reduce-scatter.5.cloned.1.call-done = f32[128,4096]{1,0:T(8,128)} async-done(((f32[512,4096]{1,0:T(8,128)}), f32[128,4096]{1,0:T(8,128)}) %reduce-scatter.5.cloned.1.call-update) | async-done | bytes 2097168 | tf_op jit(solution)/shard_map/reduce_scatter | solution.py:145
  338.2 2.7 convert_element_type.62
  (66 shorter events, 18.9 us)
Async XLA Ops:
  7.2 5.3 %copy-start = (bf16[512,512]{1,0:T(8,128)(2,1)S(1)}, bf16[512,512]{1,0:T(8,128)(2,1)}, u32[]{:S(2)}) copy-start(bf16[512,512]{1,0:T(8,128)(2,1)} %param.17) | copy-start | bytes 1572868
  7.2 85.7 %all-gather.2.cloned.1.call-start = ((), (), s32[]{:S(2)}) async-start(), calls=%async_computation.6 | async-start | bytes 8650752 | tf_op jit(solution)/shard_map/all_gather | solution.py:84
  12.5 4.0 %copy-start.2 = (bf16[512,512]{1,0:T(8,128)(2,1)S(1)}, bf16[512,512]{1,0:T(8,128)(2,1)}, u32[]{:S(2)}) copy-start(bf16[512,512]{1,0:T(8,128)(2,1)} %param.16) | copy-start | bytes 1572868
  20.8 32.1 %copy-start.6 = (s32[32,32]{1,0:T(8,128)S(1)}, s32[32,32]{1,0:T(8,128)}, u32[]{:S(2)}) copy-start(s32[32,32]{1,0:T(8,128)} %param.20) | copy-start | bytes 12292
  20.8 32.1 %copy-start.7 = (s32[32,32]{1,0:T(8,128)S(1)}, s32[32,32]{1,0:T(8,128)}, u32[]{:S(2)}) copy-start(s32[32,32]{1,0:T(8,128)} %param.21) | copy-start | bytes 12292
  20.8 32.4 %copy-start.9 = (s32[1,512]{1,0:T(1,128)S(1)}, s32[1,512]{1,0:T(1,128)}, u32[]{:S(2)}) copy-start(s32[1,512]{1,0:T(1,128)} %param.19) | copy-start | bytes 6148
  48.3 26.1 %all-to-all-start.2 = ((bf16[32,32,512]{2,1,0:T(8,128)(2,1)}), bf16[32,32,512]{2,1,0:T(8,128)(2,1)S(1)}, u32[]{:S(2)}, u32[]{:S(2)}) async-start(bf16[32,32,512]{2,1,0:T(8,128)(2,1)} %get-tuple-element.39), calls=%async_computation.2 | async-start | bytes 2097152 | tf_op jit(solution)/shard_map/all_to_all | solution.py:109
  52.7 200.9 %reduce-scatter.7.cloned.1.call-start = ((), (), s32[]{:S(2)}) async-start(), calls=%async_computation.8 | async-start | bytes 8650752
  92.9 9.3 %copy-start.4 = (bf16[32,4,2,8,256]{4,3,1,0,2:T(8,128)(2,1)S(1)}, bf16[32,4,2,8,256]{4,3,1,0,2:T(8,128)(2,1)}, u32[]{:S(2)}) copy-start(bf16[32,4,2,8,256]{4,3,1,0,2:T(8,128)(2,1)} %copy.92) | copy-start | bytes 3145732
  102.1 2.8 copy-start.3
  111.6 2.2 copy-start.10
  113.8 15.8 %copy-start.5 = (bf16[2,256,512]{2,1,0:T(8,128)(2,1)S(1)}, bf16[2,256,512]{2,1,0:T(8,128)(2,1)}, u32[]{:S(2)}) copy-start(bf16[2,256,512]{2,1,0:T(8,128)(2,1)} %fusion.26) | copy-start | bytes 1572868
  151.2 186.9 %reduce-scatter.5.cloned.1.call-start = ((), (), s32[]{:S(2)}) async-start(), calls=%async_computation.7 | async-start | bytes 10485760 | tf_op jit(solution)/shard_map/reduce_scatter | solution.py:145
  180.6 22.7 %all-to-all-start.3 = ((bf16[32,32,512]{2,1,0:T(8,128)(2,1)}), bf16[32,32,512]{2,1,0:T(8,128)(2,1)S(1)}, u32[]{:S(2)}, u32[]{:S(2)}) async-start(bf16[32,32,512]{2,1,0:T(8,128)(2,1)} %bitcast.54), calls=%async_computation.3 | async-start | bytes 2097152 | tf_op jit(solution)/shard_map/all_to_all | solution.py:120
  189.3 18.0 %copy-start.8 = (s32[1,512]{1,0:T(1,128)S(1)}, s32[1,512]{1,0:T(1,128)}, u32[]{:S(2)}) copy-start(s32[1,512]{1,0:T(1,128)} %param.18) | copy-start | bytes 6148
  203.3 29.9 %all-to-all-start.1 = ((bf16[32,32,512]{2,1,0:T(8,128)(2,1)}), bf16[32,32,512]{2,1,0:T(8,128)(2,1)S(1)}, u32[]{:S(2)}, u32[]{:S(2)}) async-start(bf16[32,32,512]{2,1,0:T(8,128)(2,1)} %bitcast.105), calls=%async_computation.1 | async-start | bytes 2097152 | tf_op jit(solution)/shard_map/all_to_all | solution.py:106
  233.1 107.7 %copy-start.1 = (bf16[512,512]{1,0:T(8,128)(2,1)S(1)}, bf16[512,512]{1,0:T(8,128)(2,1)}, u32[]{:S(2)}) copy-start(bf16[512,512]{1,0:T(8,128)(2,1)} %param.17) | copy-start | bytes 1572868
Sparse Core Ops, SparseCore 0:
  10.8 82.0 all-gather.1
  151.4 102.2 reduce-scatter.6
  256.3 81.8 reduce-scatter.4
where the time goes:
time: 348 us; the launch traced here: 347 us
  waiting for transfers between devices  173 us (50%)
  matrix products  71.3 us (20%)
  local copies, waits for them, and re-layouts  34.2 us (10%)
  blocking collectives  26.2 us (8%)
  starting transfers between devices  14.4 us (4%)
  other arithmetic  14.1 us (4%)
  between operations  14.1 us (4%)
    reduce_scatter x1, waiting for transfers between devices, per_device(): lax.psum_scatter(partial_sums, 'fsdp', scatter_dimension=0, tiled=True)  81.6 us
    all_to_all x1, blocking collectives, per_device(): lax.all_to_all(outgoing, 'dp', split_axis=0, concat_axis=0, tiled=True)  26.2 us
    all_to_all x1, waiting for transfers between devices, per_device(): lax.all_to_all(answers, 'dp', split_axis=0, concat_axis=0, tiled=True)  23.8 us
    dot_general x2, matrix products, apply_weights(): jnp.einsum('thrk,khd->trhd', weights, value_set, preferred_element_type=j...  21 us
    all_to_all x1, waiting for transfers between devices, per_device(): lax.all_to_all(grad_outgoing, 'dp', split_axis=0, concat_axis=0, tiled=True)  19.9 us
    dot_general x2, matrix products, spread_back(): jnp.einsum('thrk,trhd->khd', weights, right, preferred_element_type=jnp.f...  18 us
    unnamed x4, waiting for transfers between devices  17.5 us
    all_gather x1, waiting for transfers between devices, per_device(): piece = lax.all_gather(stacked, 'dp', axis=0, tiled=True)  17.4 us
  transfers between devices with their start and end apart: 6, of which 6 were waited for; matrix products, arithmetic and copies ran while one was open for 16% of the time, Pallas kernels for 0%

commit v1 on v0

--- a/solution.py
+++ b/solution.py
@@ -6,6 +6,11 @@
 HD = 256
 SCORE_SCALE = 0.0625
 MASKED_SCORE = -1e30
+
+
+def gather_over(shard, name, d):
+    sent = jnp.stack([shard] * lax.axis_size(name))
+    return jnp.concatenate(lax.all_to_all(sent, name, 0, 0), axis=d)
 
 
 def lookup(table, indices):
@@ -81,7 +86,7 @@
     row_count = memory.shape[0]
     depth = 2 * query.shape[0] // peer_count
     stacked = jnp.stack((key_weight, value_weight), axis=1)
-    piece = lax.all_gather(stacked, "dp", axis=0, tiled=True)
+    piece = gather_over(stacked, "dp", 0)
     columns = memory
     projected = jnp.dot(
         columns, piece.reshape(piece.shape[0], 2 * width), preferred_element_type=jnp.float32

time: 348 us -> 454 us (1.30)
  waiting for transfers between devices: 173 us -> 253 us
  local copies, waits for them, and re-layouts: 34.2 us -> 52.6 us
  starting transfers between devices: 14.4 us -> 25.2 us
    all_to_all x1 -> x2, waiting for transfers between devices: 19.9 us -> 118 us  [the longest x1 96.9 us: gather_over(): return jnp.concatenate(lax.all_to_all(sent, name, 0, 0), axis=d)]
    all_gather x1, waiting for transfers between devices: 17.4 us -> 0.02 us  [per_device(): piece = lax.all_gather(stacked, 'dp', axis=0, tiled=True)]
    unnamed x28 -> x31, local copies, waits for them, and re-layouts: 16.9 us -> 26.6 us
    another operation x1 -> x3, local copies, waits for them, and re-layouts: 0.09 us -> 8.84 us  [the longest x1 8.56 us: gather_over(): sent = jnp.stack([shard] * lax.axis_size(name))]
    all_to_all x1 -> x2, starting transfers between devices: 4.43 us -> 10.7 us  [the longest x1 6.28 us: gather_over(): return jnp.concatenate(lax.all_to_all(sent, name, 0, 0), axis=d)]
    all_to_all x1, starting transfers between devices: 5.51 us -> 10.3 us  [per_device(): lax.all_to_all(slot_grad, 'dp', split_axis=0, concat_axis=0, tiled=True)]
  transfers between devices with their start and end apart: 6 -> 7, of which waited for: 6 -> 6; matrix products, arithmetic and copies ran while one was open for 16% -> 28% of each run, Pallas kernels for 0% -> 0%
where the time goes in v1:
time: 454 us; the launch traced here: 452 us
  waiting for transfers between devices  253 us (56%)
  matrix products  70 us (15%)
  local copies, waits for them, and re-layouts  52.6 us (12%)
  blocking collectives  26.2 us (6%)
  starting transfers between devices  25.2 us (6%)
  between operations  14.1 us (3%)
  other arithmetic  11.3 us (2%)
    all_to_all x1, waiting for transfers between devices, gather_over(): return jnp.concatenate(lax.all_to_all(sent, name, 0, 0), axis=d)  96.9 us
    reduce_scatter x1, waiting for transfers between devices, per_device(): lax.psum_scatter(partial_sums, 'fsdp', scatter_dimension=0, tiled=True)  81.7 us
    unnamed x31, local copies, waits for them, and re-layouts  26.6 us
    all_to_all x1, blocking collectives, per_device(): lax.all_to_all(grad_outgoing, 'dp', split_axis=0, concat_axis=0, tiled=True)  26.2 us
    all_to_all x1, waiting for transfers between devices, per_device(): lax.all_to_all(answers, 'dp', split_axis=0, concat_axis=0, tiled=True)  22.8 us
    all_to_all x1, waiting for transfers between devices, per_device(): lax.all_to_all(outgoing, 'dp', split_axis=0, concat_axis=0, tiled=True)  21.5 us
    dot_general x2, matrix products, apply_weights(): jnp.einsum('thrk,khd->trhd', weights, value_set, preferred_element_type=j...  20.8 us
    dot_general x2, matrix products, spread_back(): jnp.einsum('thrk,trhd->khd', weights, right, preferred_element_type=jnp.f...  19.7 us
  transfers between devices with their start and end apart: 7, of which 6 were waited for; matrix products, arithmetic and copies ran while one was open for 28% of the time, Pallas kernels for 0%

profile of v1, /device:TPU:1, one launch (start us, length us, event | category | flops | bytes accessed | tf_op | source)
XLA Modules:
  0.0 452.5 jit_solution(2617094448407533233)
XLA Ops:
  12.6 4.0 gather_fusion.2
  16.6 4.0 gather_fusion
  22.0 26.2 %all_to_all.25 = bf16[32,32,512]{2,1,0:T(8,128)(2,1)S(1)} all-to-all(bf16[32,32,512]{2,1,0:T(8,128)(2,1)S(1)} %get-tuple-element.39), channel_id=1, replica_groups=mesh['dp'=32,'fsdp'=4] {'dp'}, dimensions={0} | all-to-all | bytes 2097152 | tf_op jit(solution)/shard_map/all_to_all | solution.py:114
  48.3 4.4 all-to-all-start.1
  52.9 21.5 %all-to-all-done.1 = bf16[32,32,512]{2,1,0:T(8,128)(2,1)S(1)} async-done(((bf16[32,32,512]{2,1,0:T(8,128)(2,1)}), bf16[32,32,512]{2,1,0:T(8,128)(2,1)S(1)}, u32[]{:S(2)}, u32[]{:S(2)}) %all-to-all-start.1) | async-done | bytes 1048608 | tf_op jit(solution)/shard_map/all_to_all | solution.py:105
  74.4 8.6 %stack.11 = bf16[32,128,2,512]{3,2,1,0:T(2,128)(2,1)} broadcast(bf16[128,2,512]{2,1,0:T(2,128)(2,1)S(1)} %copy.63), dimensions={1,2,3} | broadcast | bytes 8650752 | tf_op jit(solution)/shard_map/stack | solution.py:12
  82.9 6.3 %all-to-all-start = ((bf16[32,128,2,512]{3,2,1,0:T(2,128)(2,1)}), bf16[32,128,2,512]{3,2,1,0:T(2,128)(2,1)}, u32[]{:S(2)}, u32[]{:S(2)}) async-start(bf16[32,128,2,512]{3,2,1,0:T(2,128)(2,1)} %stack.11), calls=%async_computation | async-start | bytes 16777216 | tf_op jit(solution)/shard_map/all_to_all | solution.py:13
  92.1 96.9 %all-to-all-done = bf16[32,128,2,512]{3,2,1,0:T(2,128)(2,1)} async-done(((bf16[32,128,2,512]{3,2,1,0:T(2,128)(2,1)}), bf16[32,128,2,512]{3,2,1,0:T(2,128)(2,1)}, u32[]{:S(2)}, u32[]{:S(2)}) %all-to-all-start) | async-done | bytes 8388640 | tf_op jit(solution)/shard_map/all_to_all | solution.py:13
  189.0 9.3 %copy.92 = bf16[512,8,2,512]{3,1,2,0:T(8,128)(2,1)} copy(bf16[512,8,2,512]{3,2,1,0:T(2,128)(2,1)} %bitcast.56) | data formatting | bytes 16777216
  198.3 9.2 %fusion.19 = bf16[512,1024]{0,1:T(8,128)(2,1)S(1)} fusion(bf16[4096,1024]{1,0:T(8,128)(2,1)} %bitcast.98, bf16[512,4096]{1,0:T(8,128)(2,1)} %param.13), kind=kOutput, calls=%fused_computation.23 | convolution fusion | flops 4295491584 | bytes 13631488 | tf_op jit(solution)/shard_map/dot_general | solution.py:91
  211.0 3.3 fusion.46
  214.3 16.5 %fusion.27 = bf16[2,256,512]{2,1,0:T(8,128)(2,1)} fusion(f32[32,2,32,512]{3,2,0,1:T(8,128)} %bitcast.101, bf16[32,4,2,8,256]{4,3,2,1,0:T(8,128)(2,1)S(1)} %bitcast.107, f32[32,2,32,512]{3,2,0,1:T(8,128)} %get-tuple-element.46, f32[32,2,32]{2,0,1:T(8,128)S(1)} %get-tuple-element.45), kind=kOutput, calls=%fused_computation.28 | convolution fusion | flops 544475648 | bytes 9969664 | tf_op jit(solution)/shard_map/thrk,trhd->khd/dot_general | solution.py:60
  230.9 3.2 fusion.26
  234.5 6.7 %convert_bitcast_fusion = bf16[4096,1024]{0,1:T(8,128)(2,1)} fusion(bf16[512,4096]{1,0:T(8,128)(2,1)S(1)} %copy-done.11, bf16[512,512]{0,1:T(8,128)(2,1)S(1)} %bitcast.117, bf16[512,512]{0,1:T(8,128)(2,1)S(1)} %bitcast.115), kind=kOutput, calls=%fused_computation.6 | convolution fusion | flops 4301258752 | bytes 13631488 | tf_op jit(solution)/shard_map/dot_general | solution.py:138
  241.2 11.9 %copy.86 = bf16[4096,1024]{1,0:T(8,128)(2,1)} copy(bf16[4096,1024]{0,1:T(8,128)(2,1)} %convert_bitcast_fusion) | data formatting | bytes 16777216
  253.2 10.2 %fusion.32 = f32[512,4096]{1,0:T(8,128)} fusion(bf16[4096,1024]{0,1:T(8,128)(2,1)} %bitcast.97, bf16[512,512]{0,1:T(8,128)(2,1)S(1)} %bitcast.118, bf16[512,512]{0,1:T(8,128)(2,1)S(1)} %bitcast.116), kind=kOutput, calls=%fused_computation.38 | convolution fusion | flops 4297064448 | bytes 17825792 | tf_op jit(solution)/shard_map/dot_general | solution.py:147
  263.4 17.6 %fusion.20 = bf16[2,32,4,8,256]{4,3,2,1,0:T(8,128)(2,1)S(1)} fusion(bf16[512,2,256,1]{0,2,3,1:T(8,128)(2,1)S(1)} %bitcast.114, f32[32,2,32,512]{3,2,0,1:T(8,128)} %bitcast.102, f32[32,2,32,512]{3,2,0,1:T(8,128)} %get-tuple-element.46, f32[32,2,32]{2,0,1:T(8,128)S(1)} %get-tuple-element.45), kind=kOutput, calls=%fused_computation.24 | convolution fusion | flops 544737792 | bytes 9969664 | tf_op jit(solution)/shard_map/thrk,khd->trhd/dot_general | solution.py:56
  282.1 10.3 %all-to-all-start.4 = ((bf16[32,32,512]{2,1,0:T(8,128)(2,1)}), bf16[32,32,512]{2,1,0:T(8,128)(2,1)S(1)}, u32[]{:S(2)}, u32[]{:S(2)}) async-start(bf16[32,32,512]{2,1,0:T(8,128)(2,1)} %bitcast.54), calls=%async_computation.4 | async-start | bytes 2097152 | tf_op jit(solution)/shard_map/all_to_all | solution.py:125
  292.3 3.2 fusion.18
  296.6 13.0 %all-to-all-done.4 = bf16[32,32,512]{2,1,0:T(8,128)(2,1)S(1)} async-done(((bf16[32,32,512]{2,1,0:T(8,128)(2,1)}), bf16[32,32,512]{2,1,0:T(8,128)(2,1)S(1)}, u32[]{:S(2)}, u32[]{:S(2)}) %all-to-all-start.4) | async-done | bytes 1048608 | tf_op jit(solution)/shard_map/all_to_all | solution.py:125
  309.6 4.0 all-to-all-start.2
  315.7 22.8 %all-to-all-done.2 = bf16[32,32,512]{2,1,0:T(8,128)(2,1)S(1)} async-done(((bf16[32,32,512]{2,1,0:T(8,128)(2,1)}), bf16[32,32,512]{2,1,0:T(8,128)(2,1)S(1)}, u32[]{:S(2)}, u32[]{:S(2)}) %all-to-all-start.2) | async-done | bytes 1048608 | tf_op jit(solution)/shard_map/all_to_all | solution.py:111
  341.6 17.1 %reduce-scatter.7.cloned.1.call-done = bf16[128,1024]{1,0:T(8,128)(2,1)} async-done(((bf16[4096,1024]{1,0:T(8,128)(2,1)}), bf16[128,1024]{1,0:T(8,128)(2,1)}) %reduce-scatter.7.cloned.1.call-update) | async-done | bytes 262160
  361.6 81.7 %reduce-scatter.5.cloned.1.call-done = f32[128,4096]{1,0:T(8,128)} async-done(((f32[512,4096]{1,0:T(8,128)}), f32[128,4096]{1,0:T(8,128)}) %reduce-scatter.5.cloned.1.call-update) | async-done | bytes 2097168 | tf_op jit(solution)/shard_map/reduce_scatter | solution.py:150
  (73 shorter events, 26.6 us)
Async XLA Ops:
  7.2 5.4 %copy-start = (bf16[512,512]{1,0:T(8,128)(2,1)S(1)}, bf16[512,512]{1,0:T(8,128)(2,1)}, u32[]{:S(2)}) copy-start(bf16[512,512]{1,0:T(8,128)(2,1)} %param.17) | copy-start | bytes 1572868
  7.2 246.0 %all-gather.2.cloned.1.call-start = ((), (), s32[]{:S(2)}) async-start(), calls=%async_computation.7 | async-start | bytes 8650752 | tf_op jit(solution)/shard_map/all_gather | solution.py:145
  12.6 4.0 copy-start.2
  20.8 31.9 %copy-start.5 = (bf16[128,2,512]{0,2,1:T(8,128)(2,1)S(1)}, bf16[128,2,512]{0,2,1:T(8,128)(2,1)}, u32[]{:S(2)}) copy-start(bf16[128,2,512]{0,2,1:T(8,128)(2,1)} %pad_maximum_fusion.3) | copy-start | bytes 786436
  48.3 26.1 %all-to-all-start.1 = ((bf16[32,32,512]{2,1,0:T(8,128)(2,1)}), bf16[32,32,512]{2,1,0:T(8,128)(2,1)S(1)}, u32[]{:S(2)}, u32[]{:S(2)}) async-start(bf16[32,32,512]{2,1,0:T(8,128)(2,1)} %get-tuple-element.40), calls=%async_computation.1 | async-start | bytes 2097152 | tf_op jit(solution)/shard_map/all_to_all | solution.py:105
  82.9 6.5 %copy-start.7 = (s32[32,32]{1,0:T(8,128)S(1)}, s32[32,32]{1,0:T(8,128)}, u32[]{:S(2)}) copy-start(s32[32,32]{1,0:T(8,128)} %param.20) | copy-start | bytes 12292
  82.9 6.5 %copy-start.8 = (s32[32,32]{1,0:T(8,128)S(1)}, s32[32,32]{1,0:T(8,128)}, u32[]{:S(2)}) copy-start(s32[32,32]{1,0:T(8,128)} %param.21) | copy-start | bytes 12292
  82.9 6.8 %copy-start.10 = (s32[1,512]{1,0:T(1,128)S(1)}, s32[1,512]{1,0:T(1,128)}, u32[]{:S(2)}) copy-start(s32[1,512]{1,0:T(1,128)} %param.19) | copy-start | bytes 6148
  82.9 106.1 %all-to-all-start = ((bf16[32,128,2,512]{3,2,1,0:T(2,128)(2,1)}), bf16[32,128,2,512]{3,2,1,0:T(2,128)(2,1)}, u32[]{:S(2)}, u32[]{:S(2)}) async-start(bf16[32,128,2,512]{3,2,1,0:T(2,128)(2,1)} %stack.11), calls=%async_computation | async-start | bytes 16777216 | tf_op jit(solution)/shard_map/all_to_all | solution.py:13
  89.2 269.5 %reduce-scatter.7.cloned.1.call-start = ((), (), s32[]{:S(2)}) async-start(), calls=%async_computation.9 | async-start | bytes 8650752
  198.3 9.3 %copy-start.4 = (bf16[32,4,2,8,256]{4,3,1,0,2:T(8,128)(2,1)S(1)}, bf16[32,4,2,8,256]{4,3,1,0,2:T(8,128)(2,1)}, u32[]{:S(2)}) copy-start(bf16[32,4,2,8,256]{4,3,1,0,2:T(8,128)(2,1)} %copy.97) | copy-start | bytes 3145732
  207.5 2.8 copy-start.3
  230.8 3.2 copy-start.6
  230.8 3.6 copy-start.11
  253.1 190.1 %reduce-scatter.5.cloned.1.call-start = ((), (), s32[]{:S(2)}) async-start(), calls=%async_computation.8 | async-start | bytes 10485760 | tf_op jit(solution)/shard_map/reduce_scatter | solution.py:150
  282.1 27.5 %all-to-all-start.4 = ((bf16[32,32,512]{2,1,0:T(8,128)(2,1)}), bf16[32,32,512]{2,1,0:T(8,128)(2,1)S(1)}, u32[]{:S(2)}, u32[]{:S(2)}) async-start(bf16[32,32,512]{2,1,0:T(8,128)(2,1)} %bitcast.54), calls=%async_computation.4 | async-start | bytes 2097152 | tf_op jit(solution)/shard_map/all_to_all | solution.py:125
  295.5 18.1 %copy-start.9 = (s32[1,512]{1,0:T(1,128)S(1)}, s32[1,512]{1,0:T(1,128)}, u32[]{:S(2)}) copy-start(s32[1,512]{1,0:T(1,128)} %param.18) | copy-start | bytes 6148
  309.6 28.9 %all-to-all-start.2 = ((bf16[32,32,512]{2,1,0:T(8,128)(2,1)}), bf16[32,32,512]{2,1,0:T(8,128)(2,1)S(1)}, u32[]{:S(2)}, u32[]{:S(2)}) async-start(bf16[32,32,512]{2,1,0:T(8,128)(2,1)} %bitcast.108), calls=%async_computation.2 | async-start | bytes 2097152 | tf_op jit(solution)/shard_map/all_to_all | solution.py:111
  338.5 107.4 %copy-start.1 = (bf16[512,512]{1,0:T(8,128)(2,1)S(1)}, bf16[512,512]{1,0:T(8,128)(2,1)}, u32[]{:S(2)}) copy-start(bf16[512,512]{1,0:T(8,128)(2,1)} %param.17) | copy-start | bytes 1572868
Sparse Core Ops, SparseCore 0:
  10.8 82.0 all-gather.1
  253.2 105.4 reduce-scatter.6
  361.4 81.8 reduce-scatter.4
